TPU v7x, 32 devices: a whole 2x2x4 slice. The times are simulated.
32 devices in a mesh: grid: 8 (over y, x, core), ipts: 4 (over z).
Axes of the slice: x: 2, y: 2, z: 4, core: 2. Of those that a mesh axis runs over, the one named last changes fastest.
Arguments:
- orbitals: bfloat16 [16384, 1024], P(('grid', 'ipts')), may hold values from -1.1953125 to 1.1953125
- targets: bfloat16 [16384, 256], P(('grid', 'ipts')), may hold values from -6 to 6
- points: int32 [4, 1024], P('ipts', 'grid'), may hold values from 0 to 16383, as said below
- potential: bfloat16 [16384, 4096], P('grid', 'ipts'), may hold values from -0.09375 to 0.09375
Outputs:
- exchanged: bfloat16 [16384, 256], P(('grid', 'ipts'))
Inputs may be any that keep to these rules, and one draw needn't show every extreme that they name: Indices are distinct over all groups; each row of points rises strictly, and its entries k * 128 to (k + 1) * 128 - 1 lie in grid rows k * 2048 to (k + 1) * 2048 - 1.
All inputs are finite; a program needn't handle non-finite values.
Results may differ from a plain program's by a relative error of at most 0.0049.
Values may be sent and summed in bfloat16 or wider, within the bound.
A program may use at most 128 MiB of HBM per device.

v0:
```python
import functools

import jax
import jax.numpy as jnp
from jax import lax
from jax.experimental import pallas as pl
from jax.experimental.pallas import tpu as pltpu
from jax.sharding import PartitionSpec as P

MESH = pl.DeviceIdType.MESH
WIDTH = 256


def kernel(groups, slabs, pieces, orbitals, targets, points, potential, out,
           slab, orbital_values, target_values, weights, target_rows, every_group, picked, landed,
           total, leaving, arriving,
           local_sem, up_sem, down_sem, row_sem, grid_send, grid_recv, index_send, index_recv,
           pick_send, pick_recv, value_send, value_recv, sum_send, sum_recv):
    g = lax.axis_index("grid")
    z = lax.axis_index("ipts")
    rows, norb = orbitals.shape
    nj = targets.shape[1]
    count = points.shape[1]
    cut = norb // pieces

    def at(grid, group):
        return {"grid": grid, "ipts": group}

    def other(base, step, size):
        return lax.rem(base + step, size)

    own = [
        pltpu.make_async_copy(
            orbitals.at[:, pl.ds(k * cut, cut)], slab.at[z, :, pl.ds(k * cut, cut)], local_sem.at[k])
        for k in range(pieces)
    ]
    own_targets = pltpu.make_async_copy(targets, target_rows, local_sem.at[pieces])
    own_points = pltpu.make_async_copy(points, every_group.at[0], local_sem.at[pieces + 1])
    own_weights = pltpu.make_async_copy(potential, weights, local_sem.at[pieces + 2])
    own_points.start()
    for copy in own:
        copy.start()
    own_targets.start()
    own_weights.start()

    barrier = pltpu.get_barrier_semaphore()
    for step in range(1, groups):
        pl.semaphore_signal(barrier, inc=1, device_id=at(g, other(z, step, groups)), device_id_type=MESH)
    for step in range(1, slabs):
        pl.semaphore_signal(barrier, inc=1, device_id=at(other(g, step, slabs), z), device_id_type=MESH)
    pl.semaphore_wait(barrier, groups + slabs - 2)

    def line_copy(k, chunk, sem, target):
        block = slab.at[chunk, :, pl.ds(k * cut, cut)]
        return pltpu.make_async_remote_copy(
            src_ref=block, dst_ref=block, send_sem=sem, recv_sem=row_sem.at[k, chunk],
            device_id=at(g, target), device_id_type=MESH)

    def up(k, d):
        return (z - d >= 0) & (z + 1 < groups), line_copy(
            k, jnp.maximum(z - d, 0), up_sem.at[k, d], jnp.minimum(z + 1, groups - 1))

    def down(k, d):
        return (z + d < groups) & (z >= 1), line_copy(
            k, jnp.minimum(z + d, groups - 1), down_sem.at[k, d], jnp.maximum(z - 1, 0))

    def send_line(k, d):
        for valid, copy in (up(k, d), down(k, d)):
            pl.when(valid)(copy.start)

    def await_line(k, d):
        pl.when(z - d >= 0)(lambda: line_copy(k, jnp.maximum(z - d, 0), up_sem.at[k, 0], z).wait_recv())
        pl.when(z + d < groups)(
            lambda: line_copy(k, jnp.minimum(z + d, groups - 1), up_sem.at[k, 0], z).wait_recv())

    own[0].wait()
    send_line(0, 0)
    own_points.wait()
    index_copies = [
        pltpu.make_async_remote_copy(
            src_ref=every_group.at[0], dst_ref=every_group.at[step],
            send_sem=index_send.at[step - 1], recv_sem=index_recv.at[step - 1],
            device_id=at(g, other(z, step, groups)), device_id_type=MESH)
        for step in range(1, groups)
    ]
    for copy in index_copies:
        copy.start()

    slab_start = g * rows * groups

    def chosen(indices, start, length):
        place = lax.broadcasted_iota(jnp.int32, (length, count), 0) + start
        return (place == indices).astype(jnp.float32).astype(jnp.bfloat16)

    def pick(indices, start, block):
        return lax.dot_general(
            chosen(indices, start, block.shape[0]), block, (((0,), (0,)), ((), ())),
            preferred_element_type=jnp.float32)

    own_targets.wait()
    own_start = slab_start + z * rows
    pick_copies = []
    own_pick = pick(every_group[0], own_start, target_rows[...])
    for step in range(1, groups):
        index_copies[step - 1].wait()
        picked[step - 1] = pick(every_group[step], own_start, target_rows[...]).astype(jnp.bfloat16)
        copy = pltpu.make_async_remote_copy(
            src_ref=picked.at[step - 1], dst_ref=landed.at[step - 1],
            send_sem=pick_send.at[step - 1], recv_sem=pick_recv.at[step - 1],
            device_id=at(g, other(z, groups - step, groups)), device_id_type=MESH)
        copy.start()
        pick_copies.append(copy)

    place = pl.ds(pl.multiple_of(g * count, count), count)
    grid_copies = []

    def spread(ref, sends, recvs):
        copies = [
            pltpu.make_async_remote_copy(
                src_ref=ref, dst_ref=ref, send_sem=sends.at[step - 1], recv_sem=recvs.at[step - 1],
                device_id=at(other(g, step, slabs), z), device_id_type=MESH)
            for step in range(1, slabs)
        ]
        for copy in copies:
            copy.start()
        grid_copies.extend(copies)

    for s in range(pieces + groups - 1):
        for d in range(groups):
            k = s - d
            if not 0 <= k < pieces:
                continue
            if d > 0:
                await_line(k, d)
            elif k > 0:
                own[k].wait()
            if d < groups - 1 and s > 0:
                send_line(k, d)
        k = s - (groups - 1)
        if k < 0:
            continue
        columns = pl.ds(k * cut, cut)
        values = jnp.zeros((count, cut), jnp.float32)
        for chunk in range(groups):
            values += pick(every_group[0], slab_start + chunk * rows, slab[chunk, :, columns])
        orbital_values[place, columns] = values.astype(jnp.bfloat16)
        spread(orbital_values.at[place, columns], grid_send.at[k], grid_recv.at[k])
        if k == 0:
            values = own_pick
            for step in range(1, groups):
                pick_copies[step - 1].wait()
                values += landed[step - 1].astype(jnp.float32)
            target_values[place, :] = values.astype(jnp.bfloat16)
            spread(target_values.at[place, :], value_send, value_recv)

    own_weights.wait()
    for copy in grid_copies:
        copy.wait_recv()

    def add_up(chunk):
        total[...] = jnp.zeros_like(total)

        @pl.loop(0, slabs * count // WIDTH)
        def _(b):
            block = pl.ds(pl.multiple_of(b * WIDTH, WIDTH), WIDTH)
            products = lax.dot_general(
                slab[chunk], orbital_values[block, :], (((1,), (1,)), ((), ())),
                preferred_element_type=jnp.float32)
            kernel_rows = weights[pl.ds(pl.multiple_of(chunk * rows, rows), rows), block]
            weighted = (kernel_rows.astype(jnp.float32) * products).astype(jnp.bfloat16)
            total[...] += jnp.dot(weighted, target_values[block, :], preferred_element_type=jnp.float32)

    sum_copies = []
    for n, step in enumerate(range(1, groups)):
        chunk = other(z, step, groups)
        add_up(chunk)
        leaving[n] = total[...].astype(jnp.bfloat16)
        copy = pltpu.make_async_remote_copy(
            src_ref=leaving.at[n], dst_ref=arriving.at[n], send_sem=sum_send.at[n], recv_sem=sum_recv.at[n],
            device_id=at(g, chunk), device_id_type=MESH)
        copy.start()
        sum_copies.append(copy)
    add_up(z)
    summed = total[...]
    for n, copy in enumerate(sum_copies):
        copy.wait_recv()
        summed += arriving[n].astype(jnp.float32)
    out[...] = (-summed).astype(out.dtype)

    for k in range(pieces):
        for d in range(groups - 1):
            for valid, copy in (up(k, d), down(k, d)):
                pl.when(valid)(copy.wait_send)
    for copy in grid_copies + sum_copies:
        copy.wait_send()


def local(orbitals, targets, points, potential):
    groups, slabs = lax.axis_size("ipts"), lax.axis_size("grid")
    rows, norb = orbitals.shape
    nj = targets.shape[1]
    count = points.shape[1]
    pieces = max(norb // 256, 1)
    dma, bf16 = pltpu.SemaphoreType.DMA, jnp.bfloat16
    return pl.pallas_call(
        functools.partial(kernel, groups, slabs, pieces),
        out_shape=jax.ShapeDtypeStruct((rows, nj), bf16),
        in_specs=[pl.BlockSpec(memory_space=pl.ANY)] * 4,
        out_specs=pl.BlockSpec(memory_space=pltpu.VMEM),
        scratch_shapes=[
            pltpu.VMEM((groups, rows, norb), bf16),
            pltpu.VMEM((slabs * count, norb), bf16),
            pltpu.VMEM((slabs * count, nj), bf16),
            pltpu.VMEM(potential.shape, bf16),
            pltpu.VMEM((rows, nj), bf16),
            pltpu.VMEM((groups, 1, count), jnp.int32),
            pltpu.VMEM((groups - 1, count, nj), bf16),
            pltpu.VMEM((groups - 1, count, nj), bf16),
            pltpu.VMEM((rows, nj), jnp.float32),
            pltpu.VMEM((groups - 1, rows, nj), bf16),
            pltpu.VMEM((groups - 1, rows, nj), bf16),
            dma((pieces + 3,)),
            dma((pieces, groups - 1)),
            dma((pieces, groups - 1)),
            dma((pieces, groups)),
            dma((pieces, slabs - 1)),
            dma((pieces, slabs - 1)),
            dma((groups - 1,)),
            dma((groups - 1,)),
            dma((groups - 1,)),
            dma((groups - 1,)),
            dma((slabs - 1,)),
            dma((slabs - 1,)),
            dma((groups - 1,)),
            dma((groups - 1,)),
        ],
        compiler_params=pltpu.CompilerParams(
            collective_id=0, has_side_effects=True, vmem_limit_bytes=60 * 1024 * 1024),
    )(orbitals, targets, points, potential)


def solution(mesh):
    placed = (
        P(("grid", "ipts"), None),
        P(("grid", "ipts"), None),
        P("ipts", "grid"),
        P("grid", "ipts"),
    )
    return jax.shard_map(
        local, mesh=mesh, in_specs=placed, out_specs=P(("grid", "ipts"), None), check_vma=False
    )
```

profile of v0, /device:TPU:31, one launch (start us, length us, event | category | flops | bytes accessed | tf_op | source)
XLA Modules:
  0.0 113.8 jit_solution(15452731843167559843)
XLA Ops:
  0.0 112.1 %shard_map.46 = bf16[512,256]{1,0:T(8,128)(2,1)} custom-call(bf16[512,1024]{1,0:T(8,128)(2,1)} %orbitals.1, bf16[512,256]{1,0:T(8,128)(2,1)} %targets.1, s32[1,128]{1,0:T(1,128)} %points.1, bf16[2048,1024]{1,0:T(8,128)(2,1)} %potential.1), custom_call_target="tpu_custom_call" | custom-call | tf_op jit(solution)/shard_map/pallas_call | solution.py:205
  112.1 1.7 %copy.6 = bf16[512,256]{1,0:T(8,128)(2,1)} copy(bf16[512,256]{1,0:T(8,128)(2,1)} %shard_map.46) | data formatting | bytes 524288
where the time goes:
time: 114 us
  Pallas kernels  112 us (98%)
  local copies, waits for them, and re-layouts  1.67 us (1%)
    pallas_call x1, Pallas kernels, local(): pl.pallas_call(functools.partial(kernel, groups, slabs, pieces), out_shap...  112 us

commit v1 on v0

v1 whole, which is shorter than its diff:
```python
import functools

import jax
import jax.numpy as jnp
from jax import lax
from jax.experimental import pallas as pl
from jax.experimental.pallas import tpu as pltpu
from jax.sharding import PartitionSpec as P

MESH = pl.DeviceIdType.MESH
LANES = 128
WIDTH = 1024
SPLIT = 2
EARLY = 4
F32, BF16 = jnp.float32, jnp.bfloat16


class Names:
    def __init__(self, size):
        self.size, self.known = size, {}

    def __getitem__(self, name):
        number = self.known.setdefault(name, len(self.known))
        assert number < self.size
        return number


def kernel(groups, slabs, orbitals, targets, points, potential, out,
           slab, values, target_values, weights, lent, target_rows, index, hot, far_hot,
           early_out, early_near, early_in, leaving, arriving, crossing, kept, kept_end,
           local_sem, send_sem, recv_sem, plane_send, plane_recv):
    g = lax.axis_index("grid")
    z = lax.axis_index("ipts")
    side = z // 2
    q = z + side * (groups - 1 - 2 * z)
    inward, outward = z + 1 - 2 * side, z - 1 + 2 * side
    rows, norb = orbitals.shape
    nj = targets.shape[1]
    count = points.shape[1]
    total = slabs * count
    lanes = slabs // 2
    partner = g + 1 - 2 * lax.rem(g, 2)
    early = norb // EARLY
    tail = norb - early
    pieces = tail // LANES
    sub = rows // SPLIT
    width = min(WIDTH, total)
    names = Names(send_sem.shape[0])
    sent = []

    def where(block):
        return block + side * (groups - 1 - 2 * block)

    def cols(k):
        return pl.ds(k * LANES, LANES)

    last = pl.ds(tail, early)

    def place(slab_index):
        return pl.ds(pl.multiple_of(slab_index * count, count), count)

    def peer(step):
        return lax.rem(g + 2 * step, slabs)

    def source(base, step):
        return lax.rem(base + slabs - 2 * step, slabs)

    def send(name, src, dst, target):
        copy = pltpu.make_async_remote_copy(
            src_ref=src, dst_ref=dst, send_sem=send_sem.at[names[name]], recv_sem=recv_sem.at[names[name]],
            device_id={"grid": g, "ipts": target}, device_id_type=MESH)
        copy.start()
        sent.append(copy)

    def receive(name, dst):
        pltpu.make_async_remote_copy(
            src_ref=dst, dst_ref=dst, send_sem=send_sem.at[names[name]], recv_sem=recv_sem.at[names[name]],
            device_id={"grid": g, "ipts": z}, device_id_type=MESH).wait_recv()

    def across(ref, item, way, target):
        return pltpu.make_async_remote_copy(
            src_ref=ref, dst_ref=ref, send_sem=plane_send.at[item, way], recv_sem=plane_recv.at[item, way],
            device_id={"grid": target, "ipts": z}, device_id_type=MESH)

    def spread(item, view):
        for step in range(1, lanes):
            copy = across(view(place(g)), item, step, peer(step))
            copy.start()
            sent.append(copy)
        copy = across(view(place(g)), item, 0, partner)
        copy.start()
        sent.append(copy)

    def forward(item, view):
        for step in range(1, lanes):
            block = view(place(source(g, step)))
            across(block, item, step, g).wait_recv()
            copy = across(block, item, lanes + step, partner)
            copy.start()
            sent.append(copy)

    def gathered(item, view):
        across(view(place(partner)), item, 0, g).wait_recv()
        for step in range(1, lanes):
            across(view(place(source(partner, step))), item, lanes + step, g).wait_recv()

    def contribution(block, half, slot, kernel_rows):
        part = pl.ds(half * sub, sub)
        acc = None
        for start in range(0, total, width):
            some = pl.ds(start, width)
            products = lax.dot_general(
                slab[block, part, :], values[slot, some, :], (((1,), (1,)), ((), ())),
                preferred_element_type=F32)
            weighted = (kernel_rows[part, some].astype(F32) * products).astype(BF16)
            term = jnp.dot(weighted, target_values[slot, some, :], preferred_element_type=F32)
            acc = term if acc is None else acc + term
        return acc

    own_rows = pltpu.make_async_copy(orbitals, slab.at[q], local_sem.at[0])
    own_targets = pltpu.make_async_copy(targets, target_rows.at[q], local_sem.at[1])
    own_points = pltpu.make_async_copy(points, index.at[q], local_sem.at[2])
    own_weights = [
        pltpu.make_async_copy(
            potential.at[pl.ds(pl.multiple_of(where(block) * rows, rows), rows), :], weights.at[block],
            local_sem.at[3 + block])
        for block in range(groups)
    ]
    own_points.start()
    own_rows.start()
    own_targets.start()
    for copy in own_weights:
        copy.start()

    barrier = pltpu.get_barrier_semaphore()

    def greet(grid, group):
        pl.semaphore_signal(barrier, inc=1, device_id={"grid": grid, "ipts": group}, device_id_type=MESH)

    greet(g, inward)
    pl.when(q > 0)(lambda: greet(g, outward))
    greet(partner, z)
    for step in range(1, lanes):
        greet(peer(step), z)
    pl.semaphore_wait(barrier, lanes + 1 + q)

    def finish():
        for copy in sent:
            copy.wait_send()
        sent.clear()

    halves = range(SPLIT)

    def end():
        own_points.wait()
        send("index", index.at[0], index.at[0], inward)
        send("early rows", orbitals.at[:, last], slab.at[0, :, last], inward)
        send("targets", targets, target_rows.at[0], inward)
        for k in range(pieces):
            send(("end", k), orbitals.at[:, cols(k)], slab.at[0, :, cols(k)], inward)
        for half in halves:
            part = pl.ds(pl.multiple_of(where(1) * rows + half * sub, sub), sub)
            send(("lent", half), potential.at[part, :], lent.at[pl.ds(half * sub, sub), :], inward)

        views = [lambda p: values.at[0, p, last]]
        views += [lambda p, k=k: values.at[0, p, cols(k)] for k in range(pieces)]
        views += [lambda p: target_values.at[0, p, :]]
        order = [0, pieces + 1] + list(range(1, pieces + 1))
        for n, item in enumerate(order):
            receive(("value", item), views[item](place(g)))
            spread(item, views[item])
            if n > 0:
                forward(order[n - 1], views[order[n - 1]])
        forward(order[-1], views[order[-1]])
        own_rows.wait()
        own_targets.wait()
        for copy in own_weights:
            copy.wait()
        for k in range(pieces):
            receive(("out", 2, k), slab.at[2, :, cols(k)])
            receive(("out", 3, k), slab.at[3, :, cols(k)])
        for item in order:
            gathered(item, views[item])
        for half in halves:
            part = pl.ds(half * sub, sub)
            for block in (3, 2):
                receive(("out rows", block, half), slab.at[block, part, last])
                leaving[block - 2, part, :] = contribution(block, half, 0, weights.at[block]).astype(BF16)
                send(("sum", block, half), leaving.at[block - 2, part, :], arriving.at[block - 2, part, :], inward)
        for half in halves:
            kept[pl.ds(half * sub, sub), :] = contribution(0, half, 0, weights.at[0])
        for half in halves:
            part = pl.ds(half * sub, sub)
            receive(("end sum", half), arriving.at[0, part, :])
            out[part, :] = (-(kept[part, :] + arriving[0, part, :].astype(F32))).astype(out.dtype)
        finish()

    def inner():
        own_points.wait()
        send("index in", index.at[1], index.at[2], inward)
        for k in range(pieces - 1):
            send(("own", k), orbitals.at[:, cols(k)], slab.at[2, :, cols(k)], inward)
        receive("index", index.at[0])
        send("index end", index.at[0], index.at[3], inward)

        def relay(k):
            receive(("own", k), slab.at[2, :, cols(k)])
            send(("out", 2, k), slab.at[2, :, cols(k)], slab.at[2, :, cols(k)], outward)

        def cross(k):
            receive(("end", k), slab.at[0, :, cols(k)])
            send(("end in", k), slab.at[0, :, cols(k)], slab.at[3, :, cols(k)], inward)

        def mark(ref, pair, blocks):
            lane = lax.broadcasted_iota(jnp.int32, (count, LANES), 1)
            for n, group in enumerate(pair):
                wide = jnp.broadcast_to(index[group], (LANES, count)).T
                for block in range(blocks):
                    start = (g * groups + where(block)) * rows
                    for c in range(rows // LANES):
                        chosen = (wide == lane + (start + c * LANES)).astype(F32).astype(BF16)
                        ref[pl.ds(n * count, count), pl.ds(block * rows + c * LANES, LANES)] = chosen

        def pick(ref, blocks, rows_of):
            return sum(
                jnp.dot(ref[:, pl.ds(block * rows, rows)], rows_of(block), preferred_element_type=F32)
                for block in range(blocks))

        mark(hot, (1, 0), groups)
        ahead = max(pieces - 2, 0)
        for k in range(ahead):
            relay(k)
        receive("index in", index.at[2])
        receive("index end", index.at[3])
        mark(far_hot, (2, 3), 2)
        own_rows.wait()
        own_targets.wait()
        receive("early rows", slab.at[0, :, last])
        receive("targets", target_rows.at[0])
        early_out[:, pl.ds(0, early)] = pick(far_hot, 2, lambda b: slab[b, :, last]).astype(BF16)
        early_out[:, pl.ds(early, nj)] = pick(far_hot, 2, lambda b: target_rows[b]).astype(BF16)
        send("early", early_out, early_in, inward)
        early_near[:, pl.ds(0, early)] = pick(hot, 2, lambda b: slab[b, :, last]).astype(BF16)
        early_near[:, pl.ds(early, nj)] = pick(hot, 2, lambda b: target_rows[b]).astype(BF16)
        for k in range(ahead, pieces - 1):
            relay(k)
        cross(0)
        send(("own", pieces - 1), orbitals.at[:, cols(pieces - 1)], slab.at[2, :, cols(pieces - 1)], inward)

        views = [lambda p: values.at[:, p, last]]
        views += [lambda p, k=k: values.at[:, p, cols(k)] for k in range(pieces)]
        views += [lambda p: target_values.at[:, p, :]]

        receive("early", early_in)
        found = early_near[...].astype(F32) + early_in[...].astype(F32)
        for n in range(2):
            part = slice(n * count, (n + 1) * count)
            values[n, place(g), last] = found[part, :early].astype(BF16)
            target_values[n, place(g), :] = found[part, early:].astype(BF16)
        send(("value", 0), values.at[1, place(g), last], values.at[0, place(g), last], outward)
        send(("value", pieces + 1), target_values.at[1, place(g), :], target_values.at[0, place(g), :], outward)
        spread(0, views[0])
        spread(pieces + 1, views[pieces + 1])
        ready = 1

        order = [0, pieces + 1]
        for k in range(pieces):
            while ready < min(k + 3, pieces):
                cross(ready)
                ready += 1
                if ready == pieces:
                    for half in halves:
                        part = pl.ds(half * sub, sub)
                        for block in (0, 1):
                            send(("rows in", 3 - block, half), slab.at[block, part, last],
                                 slab.at[3 - block, part, last], inward)
            if k == 0:
                relay(pieces - 1)
            receive(("end in", k), slab.at[3, :, cols(k)])
            send(("out", 3, k), slab.at[3, :, cols(k)], slab.at[3, :, cols(k)], outward)
            found = pick(hot, groups, lambda b: slab[b, :, cols(k)])
            for n in range(2):
                values[n, place(g), cols(k)] = found[n * count:(n + 1) * count].astype(BF16)
            send(("value", k + 1), values.at[1, place(g), cols(k)], values.at[0, place(g), cols(k)], outward)
            spread(k + 1, views[k + 1])
            for item in order:
                forward(item, views[item])
            order = [k + 1]

        def pass_on(half):
            part = pl.ds(half * sub, sub)
            for block in (3, 2):
                receive(("rows in", block, half), slab.at[block, part, last])
                send(("out rows", block, half), slab.at[block, part, last], slab.at[block, part, last], outward)

        pass_on(0)
        forward(pieces, views[pieces])
        for half in halves[1:]:
            pass_on(half)
        for copy in own_weights:
            copy.wait()
        for item in range(pieces + 2):
            gathered(item, views[item])
        for half in halves:
            part = pl.ds(half * sub, sub)
            for block in (3, 2):
                mine = contribution(block, half, 0, weights.at[block])
                receive(("sum", block, half), arriving.at[block - 2, part, :])
                leaving[block - 2, part, :] = (mine + arriving[block - 2, part, :].astype(F32)).astype(BF16)
                send(("sum in", block, half), leaving.at[block - 2, part, :], crossing.at[3 - block, part, :], inward)
        for half in halves:
            kept_end[pl.ds(half * sub, sub), :] = contribution(0, half, 0, weights.at[0])
        for half in halves:
            part = pl.ds(half * sub, sub)
            receive(("sum in", 3, half), crossing.at[0, part, :])
            leaving[2, part, :] = (kept_end[part, :] + crossing[0, part, :].astype(F32)).astype(BF16)
            send(("end sum", half), leaving.at[2, part, :], arriving.at[0, part, :], outward)
            kept[part, :] = contribution(1, half, 0, weights.at[1])
            receive(("lent", half), lent.at[part, :])
            kept[part, :] += contribution(1, half, 1, lent)
        for half in halves:
            part = pl.ds(half * sub, sub)
            receive(("sum in", 2, half), crossing.at[1, part, :])
            out[part, :] = (-(kept[part, :] + crossing[1, part, :].astype(F32))).astype(out.dtype)
        finish()

    pl.when(q == 0)(end)
    pl.when(q == 1)(inner)


def local(orbitals, targets, points, potential):
    groups, slabs = lax.axis_size("ipts"), lax.axis_size("grid")
    assert groups == 4 and slabs % 2 == 0
    rows, norb = orbitals.shape
    nj = targets.shape[1]
    count = points.shape[1]
    early = norb // EARLY
    pieces = (norb - early) // LANES
    transfers = 12 + 6 * pieces + 20 * SPLIT
    dma = pltpu.SemaphoreType.DMA
    return pl.pallas_call(
        functools.partial(kernel, groups, slabs),
        out_shape=jax.ShapeDtypeStruct((rows, nj), BF16),
        in_specs=[pl.BlockSpec(memory_space=pl.ANY)] * 4,
        out_specs=pl.BlockSpec(memory_space=pltpu.VMEM),
        scratch_shapes=[
            pltpu.VMEM((groups, rows, norb), BF16),
            pltpu.VMEM((2, slabs * count, norb), BF16),
            pltpu.VMEM((2, slabs * count, nj), BF16),
            pltpu.VMEM((groups, rows, slabs * count), BF16),
            pltpu.VMEM((rows, slabs * count), BF16),
            pltpu.VMEM((2, rows, nj), BF16),
            pltpu.VMEM((groups, 1, count), jnp.int32),
            pltpu.VMEM((2 * count, groups * rows), BF16),
            pltpu.VMEM((2 * count, 2 * rows), BF16),
            pltpu.VMEM((2 * count, early + nj), BF16),
            pltpu.VMEM((2 * count, early + nj), BF16),
            pltpu.VMEM((2 * count, early + nj), BF16),
            pltpu.VMEM((3, rows, nj), BF16),
            pltpu.VMEM((2, rows, nj), BF16),
            pltpu.VMEM((2, rows, nj), BF16),
            pltpu.VMEM((rows, nj), F32),
            pltpu.VMEM((rows, nj), F32),
            dma((3 + groups,)),
            dma((transfers,)),
            dma((transfers,)),
            dma((pieces + 2, slabs)),
            dma((pieces + 2, slabs)),
        ],
        compiler_params=pltpu.CompilerParams(
            collective_id=0, has_side_effects=True, vmem_limit_bytes=63 * 1024 * 1024),
    )(orbitals, targets, points, potential)


def solution(mesh):
    placed = (
        P(("grid", "ipts"), None),
        P(("grid", "ipts"), None),
        P("ipts", "grid"),
        P("grid", "ipts"),
    )
    return jax.shard_map(
        local, mesh=mesh, in_specs=placed, out_specs=P(("grid", "ipts"), None), check_vma=False
    )
```

time: 114 us -> 97 us (0.85)
  the two profiles are of different devices: /device:TPU:31 before, /device:TPU:0 now
where the time goes in v1:
time: 97 us; the launch traced here: 96.8 us
  Pallas kernels  95.2 us (98%)
  local copies, waits for them, and re-layouts  1.67 us (2%)
    pallas_call x1, Pallas kernels, local(): pl.pallas_call(functools.partial(kernel, groups, slabs), out_shape=jax.Sh...  95.2 us

profile of v1, /device:TPU:0, one launch (start us, length us, event | category | flops | bytes accessed | tf_op | source)
XLA Modules:
  0.0 96.8 jit_solution(6563542451401700825)
XLA Ops:
  0.0 95.2 %shard_map.46 = bf16[512,256]{1,0:T(8,128)(2,1)} custom-call(bf16[512,1024]{1,0:T(8,128)(2,1)} %orbitals.1, bf16[512,256]{1,0:T(8,128)(2,1)} %targets.1, s32[1,128]{1,0:T(1,128)} %points.1, bf16[2048,1024]{1,0:T(8,128)(2,1)} %potential.1), custom_call_target="tpu_custom_call" | custom-call | tf_op jit(solution)/shard_map/pallas_call | solution.py:341
  95.2 1.7 %copy.6 = bf16[512,256]{1,0:T(8,128)(2,1)} copy(bf16[512,256]{1,0:T(8,128)(2,1)} %shard_map.46) | data formatting | bytes 524288

commit v2 on v1

v2 whole, which is shorter than its diff:
```python
import functools

import jax
import jax.numpy as jnp
from jax import lax
from jax.experimental import pallas as pl
from jax.experimental.pallas import tpu as pltpu
from jax.sharding import PartitionSpec as P

MESH = pl.DeviceIdType.MESH
LANES = 128
WIDTH = 1024
SPLIT = 2
EARLY = 4
SORTS = ("index", "slab", "targets", "lent", "near", "early", "values", "target values", "sums")
F32, BF16 = jnp.float32, jnp.bfloat16


class Names:
    def __init__(self, size):
        self.size, self.known = size, ({}, {})

    def __getitem__(self, key):
        kind, name = key
        number = self.known[kind].setdefault(name, len(self.known[kind]))
        assert number < self.size
        return number


def kernel(groups, slabs, orbitals, targets, points, potential, out,
           slab, values, target_values, weights, lent, target_rows, index, hot, far_hot,
           early_out, early_near, early_in, near_out, near_in, leaving, arriving, crossing, kept,
           local_sem, send_sem, recv_sem, plane_send, plane_recv, partner_recv):
    g = lax.axis_index("grid")
    z = lax.axis_index("ipts")
    side = z // 2
    q = z + side * (groups - 1 - 2 * z)
    inward, outward = z + 1 - 2 * side, z - 1 + 2 * side
    rows, norb = orbitals.shape
    nj = targets.shape[1]
    count = points.shape[1]
    total = slabs * count
    lanes = slabs // 2
    lane, core = g // 2, lax.rem(g, 2)
    partner = g + 1 - 2 * core
    bits = [1 << n for n in range(lanes.bit_length() - 1)]
    orders = (bits, bits[::-1])
    early = norb // EARLY
    tail = norb - early
    pieces = tail // LANES
    sub = rows // SPLIT
    quarter = sub // 2
    width = min(WIDTH, total)
    names = Names(recv_sem.shape[0])

    def where(block):
        return block + side * (groups - 1 - 2 * block)

    def cols(k):
        return pl.ds(k * LANES, LANES)

    last = pl.ds(tail, early)

    def place(slab_index):
        return pl.ds(pl.multiple_of(slab_index * count, count), count)

    def flipped(mask, of_core):
        there = lane
        for bit in bits:
            if mask & bit:
                there = there + bit - 2 * bit * lax.rem(lane // bit, 2)
        return 2 * there + of_core

    def send(kind, name, sort, src, dst, target):
        pltpu.make_async_remote_copy(
            src_ref=src, dst_ref=dst, send_sem=send_sem.at[SORTS.index(sort)], recv_sem=recv_sem.at[names[kind, name]],
            device_id={"grid": g, "ipts": target}, device_id_type=MESH).start()

    def receive(kind, name, dst):
        pltpu.make_async_copy(dst, dst, recv_sem.at[names[kind, name]]).wait()

    def left(sort, *views):
        for view in views:
            pltpu.make_async_copy(view, view, send_sem.at[SORTS.index(sort)]).wait()

    wide = pieces + 1

    def pass_to(block, item, way, target):
        recv = partner_recv.at[item // wide] if way is None else plane_recv.at[item, way - 1]
        pltpu.make_async_remote_copy(
            src_ref=block, dst_ref=block, send_sem=plane_send.at[item // wide], recv_sem=recv,
            device_id={"grid": target, "ipts": z}, device_id_type=MESH).start()

    def ways(mask, slots):
        if mask in bits:
            return [(mask, None)]
        return [(mask + slot * lanes, slot) for slot in range(slots)]

    def spread(item, view, slots):
        for bit in bits:
            pass_to(view(None, place(g)), item, bit, flipped(bit, core))
        pass_to(view(None, place(g)), item, None, partner)

    def forward(item, view, slots, single):
        masks = [m for m in range(1, lanes) if (m in bits) == single]
        for mask in sorted(masks, key=lambda m: m.bit_count()):
            for way, slot in ways(mask, slots):
                block = view(slot, place(flipped(mask, core)))
                pltpu.make_async_copy(block, block, plane_recv.at[item, way - 1]).wait()
                for n in range(slots) if slot is None else (slot,):
                    order = orders[n]
                    top = max(order.index(bit) for bit in bits if mask & bit)
                    for bit in order[top + 1:]:
                        pass_to(view(n, place(flipped(mask, core))), item, (mask | bit) + n * lanes, flipped(bit, core))
                pass_to(block, item, None, partner)

    def all_of(blocks, pick):
        several = pl.ds(0, blocks * count)
        return (values.at[pick, several, :], target_values.at[pick, several, :])

    def gathered(pick):
        for n, view in enumerate(all_of(lanes, pick)):
            pltpu.make_async_copy(view, view, partner_recv.at[n]).wait()

    def passed(pick):
        for n, view in enumerate(all_of(slabs - 1, pick)):
            pltpu.make_async_copy(view, view, plane_send.at[n]).wait()

    def contribution(block, half, slot, kernel_rows):
        part = pl.ds(half * sub, sub)
        acc = None
        for start in range(0, total, width):
            some = pl.ds(start, width)
            products = lax.dot_general(
                slab[block, part, :], values[slot, some, :], (((1,), (1,)), ((), ())),
                preferred_element_type=F32)
            weighted = (kernel_rows[part, some].astype(F32) * products).astype(BF16)
            term = jnp.dot(weighted, target_values[slot, some, :], preferred_element_type=F32)
            acc = term if acc is None else acc + term
        return acc

    own_rows = pltpu.make_async_copy(orbitals, slab.at[q], local_sem.at[0])
    own_targets = pltpu.make_async_copy(targets, target_rows.at[q], local_sem.at[1])
    own_points = pltpu.make_async_copy(points, index.at[q], local_sem.at[2])
    own_weights = [
        pltpu.make_async_copy(
            potential.at[pl.ds(pl.multiple_of(where(block) * rows, rows), rows), :], weights.at[block],
            local_sem.at[3 + block])
        for block in range(groups)
    ]
    own_points.start()
    own_rows.start()
    own_targets.start()
    for copy in own_weights:
        copy.start()

    barrier = pltpu.get_barrier_semaphore()

    def greet(grid, group):
        pl.semaphore_signal(barrier, inc=1, device_id={"grid": grid, "ipts": group}, device_id_type=MESH)

    greet(g, inward)
    pl.when(q > 0)(lambda: greet(g, outward))
    greet(partner, z)
    for bit in bits:
        greet(flipped(bit, core), z)
    pl.semaphore_wait(barrier, len(bits) + 2 + q)

    halves = range(SPLIT)

    quarters = [(2 * half, 2 * half + 1) for half in halves]

    def few(n):
        return pl.ds(n * quarter, quarter)

    def mark(ref, marked, blocks):
        spot = lax.broadcasted_iota(jnp.int32, (count, LANES), 1)
        for n, group in enumerate(marked):
            wanted = jnp.broadcast_to(index[group], (LANES, count)).T
            for m, block in enumerate(blocks):
                start = (g * groups + where(block)) * rows
                for c in range(rows // LANES):
                    chosen = (wanted == spot + (start + c * LANES)).astype(F32).astype(BF16)
                    ref[pl.ds(n * count, count), pl.ds(m * rows + c * LANES, LANES)] = chosen

    def pick(marks, blocks, rows_of):
        return sum(
            jnp.dot(marks[:, pl.ds(m * rows, rows)], rows_of(block), preferred_element_type=F32)
            for m, block in enumerate(blocks))

    def end():
        own_points.wait()
        send(1, "index", "index", index.at[0], index.at[0], inward)
        send(1, "early rows", "slab", orbitals.at[:, last], slab.at[0, :, last], inward)
        send(1, "targets", "targets", targets, target_rows.at[0], inward)
        for k in range(pieces):
            send(1, ("end", k), "slab", orbitals.at[:, cols(k)], slab.at[0, :, cols(k)], inward)
        for half in halves:
            part = pl.ds(pl.multiple_of(where(1) * rows + half * sub, sub), sub)
            send(1, ("lent", half), "lent", potential.at[part, :], lent.at[pl.ds(half * sub, sub), :], inward)

        views = [lambda n, p: values.at[0, p, last]]
        views += [lambda n, p, k=k: values.at[0, p, cols(k)] for k in range(pieces)]
        views += [lambda n, p: target_values.at[0, p, :]]
        marks = hot.at[pl.ds(0, count), :]
        mark(marks, (0,), (0, 2, 3))
        own_rows.wait()
        receive(0, "near", near_in)
        for item in (0, wide):
            receive(0, ("value", item), views[item](0, place(g)))
            spread(item, views[item], 1)
        before, older = [0, wide], []
        for k in range(pieces):
            for block in (2, 3):
                receive(0, ("out", block, k), slab.at[block, :, cols(k)])
            found = pick(marks, (0, 2, 3), lambda block: slab[block, :, cols(k)])
            values[0, place(g), cols(k)] = (found + near_in[:, cols(k)].astype(F32)).astype(BF16)
            spread(k + 1, views[k + 1], 1)
            for item in before:
                forward(item, views[item], 1, True)
            for item in older:
                forward(item, views[item], 1, False)
            before, older = [k + 1], before
        for item in before:
            forward(item, views[item], 1, True)
        for item in older + before:
            forward(item, views[item], 1, False)
        own_targets.wait()
        for copy in own_weights:
            copy.wait()
        gathered(0)
        for block in (3, 2):
            for half in halves:
                part = pl.ds(half * sub, sub)
                receive(0, ("out rows", block, half), slab.at[block, part, last])
                leaving[block - 2, part, :] = contribution(block, half, 0, weights.at[block]).astype(BF16)
                for n in quarters[half]:
                    send(1, ("sum", block, n), "sums", leaving.at[block - 2, few(n), :],
                         arriving.at[block - 2, few(n), :], inward)
        for half in halves:
            kept[0, pl.ds(half * sub, sub), :] = contribution(0, half, 0, weights.at[0])
        for n in range(2 * SPLIT):
            receive(0, ("end sum", n), arriving.at[0, few(n), :])
            out[few(n), :] = (-(kept[0, few(n), :] + arriving[0, few(n), :].astype(F32))).astype(out.dtype)
        left("index", index.at[0])
        left("slab", slab.at[0])
        left("targets", target_rows.at[0])
        left("lent", lent)
        left("sums", leaving.at[pl.ds(0, 2)])
        passed(0)

    def inner():
        both = pl.ds(0, 2)
        own_points.wait()
        send(1, "index in", "index", index.at[1], index.at[2], inward)

        def own(k):
            send(1, ("own", k), "slab", orbitals.at[:, cols(k)], slab.at[2, :, cols(k)], inward)

        own(0)
        receive(1, "index", index.at[0])
        send(1, "index end", "index", index.at[0], index.at[3], inward)
        for k in range(1, pieces):
            own(k)

        def relay(block, k):
            send(0, ("out", block, k), "slab", slab.at[block, :, cols(k)], slab.at[block, :, cols(k)], outward)

        def relay_own(k):
            receive(1, ("own", k), slab.at[2, :, cols(k)])
            relay(2, k)

        def cross(k):
            receive(1, ("end", k), slab.at[0, :, cols(k)])
            send(1, ("end in", k), "slab", slab.at[0, :, cols(k)], slab.at[3, :, cols(k)], inward)

        mark(hot, (1, 0), range(groups))
        own_rows.wait()
        near_out[...] = jnp.dot(
            hot[pl.ds(count, count), pl.ds(rows, rows)], slab[1, :, pl.ds(0, tail)],
            preferred_element_type=F32).astype(BF16)
        send(0, "near", "near", near_out, near_in, outward)
        ahead = max(pieces - 2, 0)
        for k in range(ahead):
            relay_own(k)
        receive(1, "index in", index.at[2])
        receive(1, "index end", index.at[3])
        mark(far_hot, (2, 3), (0, 1))
        own_targets.wait()
        receive(1, "early rows", slab.at[0, :, last])
        receive(1, "targets", target_rows.at[0])
        early_out[:, pl.ds(0, early)] = pick(far_hot, (0, 1), lambda b: slab[b, :, last]).astype(BF16)
        early_out[:, pl.ds(early, nj)] = pick(far_hot, (0, 1), lambda b: target_rows[b]).astype(BF16)
        send(1, "early", "early", early_out, early_in, inward)
        early_near[:, pl.ds(0, early)] = pick(hot, (0, 1), lambda b: slab[b, :, last]).astype(BF16)
        early_near[:, pl.ds(early, nj)] = pick(hot, (0, 1), lambda b: target_rows[b]).astype(BF16)
        for k in range(ahead, pieces):
            relay_own(k)
        ready = min(pieces, 3)
        for k in range(ready):
            cross(k)

        views = [lambda n, p: values.at[both if n is None else n, p, last]]
        views += [lambda n, p, k=k: values.at[both if n is None else n, p, cols(k)] for k in range(pieces)]
        views += [lambda n, p: target_values.at[both if n is None else n, p, :]]

        receive(1, "early", early_in)
        found = early_near[...].astype(F32) + early_in[...].astype(F32)
        for n in range(2):
            part = slice(n * count, (n + 1) * count)
            values[n, place(g), last] = found[part, :early].astype(BF16)
            target_values[n, place(g), :] = found[part, early:].astype(BF16)
        send(0, ("value", 0), "values", values.at[1, place(g), last], values.at[0, place(g), last], outward)
        send(0, ("value", wide), "target values", target_values.at[1, place(g), :],
             target_values.at[0, place(g), :], outward)
        spread(0, views[0], 2)
        spread(wide, views[wide], 2)

        def rows_in():
            for block in (0, 1):
                for half in halves:
                    part = pl.ds(half * sub, sub)
                    send(1, ("rows in", 3 - block, half), "slab", slab.at[block, part, last],
                         slab.at[3 - block, part, last], inward)

        before, older = [0, wide], []
        for k in range(pieces):
            while ready < min(pieces, 5 + k):
                cross(ready)
                ready += 1
                if ready == pieces:
                    rows_in()
            receive(1, ("end in", k), slab.at[3, :, cols(k)])
            relay(3, k)
            found = pick(hot, range(groups), lambda b: slab[b, :, cols(k)])
            for n in range(2):
                values[n, place(g), cols(k)] = found[n * count:(n + 1) * count].astype(BF16)
            spread(k + 1, views[k + 1], 2)
            for item in before:
                forward(item, views[item], 2, True)
            for item in older:
                forward(item, views[item], 2, False)
            before, older = [k + 1], before

        def pass_on(block):
            for half in halves:
                part = pl.ds(half * sub, sub)
                receive(1, ("rows in", block, half), slab.at[block, part, last])
                send(0, ("out rows", block, half), "slab", slab.at[block, part, last],
                     slab.at[block, part, last], outward)

        pass_on(3)
        for item in before:
            forward(item, views[item], 2, True)
        for item in older + before:
            forward(item, views[item], 2, False)
        pass_on(2)
        for copy in own_weights:
            copy.wait()
        gathered(both)

        def keep(block, half, slot, kernel_rows):
            part = pl.ds(half * sub, sub)
            kept[block, part, :] = contribution(block, half, slot, kernel_rows)

        def sums(block, half):
            for n in quarters[half]:
                receive(1, ("sum", block, n), arriving.at[block - 2, few(n), :])
                leaving[block - 2, few(n), :] = (
                    kept[block, few(n), :] + arriving[block - 2, few(n), :].astype(F32)).astype(BF16)
                send(1, ("sum in", block, n), "sums", leaving.at[block - 2, few(n), :],
                     crossing.at[3 - block, few(n), :], inward)

        def end_sums(half):
            for n in quarters[half]:
                receive(1, ("sum in", 3, n), crossing.at[0, few(n), :])
                leaving[2, few(n), :] = (kept[0, few(n), :] + crossing[0, few(n), :].astype(F32)).astype(BF16)
                send(0, ("end sum", n), "sums", leaving.at[2, few(n), :], arriving.at[0, few(n), :], outward)

        def near(half):
            part = pl.ds(half * sub, sub)
            keep(1, half, 0, weights.at[1])
            receive(1, ("lent", half), lent.at[part, :])
            kept[1, part, :] += contribution(1, half, 1, lent)

        for block in (3, 2):
            for half in halves:
                keep(block, half, 0, weights.at[block])
                if half > 0:
                    sums(block, half - 1)
            if block == 2:
                for half in halves:
                    keep(0, half, 0, weights.at[0])
            for half in halves:
                if block == 2:
                    end_sums(half)
            sums(block, SPLIT - 1)
        for half in halves:
            near(half)
        for n in range(2 * SPLIT):
            receive(1, ("sum in", 2, n), crossing.at[1, few(n), :])
            out[few(n), :] = (-(kept[1, few(n), :] + crossing[1, few(n), :].astype(F32))).astype(out.dtype)
        left("index", index.at[both])
        left("slab", slab)
        left("near", near_out)
        left("early", early_out)
        left("values", values.at[0, pl.ds(0, count), last])
        left("target values", target_values.at[0, pl.ds(0, count), :])
        left("sums", leaving)
        passed(both)

    pl.when(q == 0)(end)
    pl.when(q == 1)(inner)


def local(orbitals, targets, points, potential):
    groups, slabs = lax.axis_size("ipts"), lax.axis_size("grid")
    assert groups == 4 and slabs.bit_count() == 1
    rows, norb = orbitals.shape
    nj = targets.shape[1]
    count = points.shape[1]
    early = norb // EARLY
    pieces = (norb - early) // LANES
    transfers = 6 + 3 * pieces + 11 * SPLIT
    lanes = slabs // 2
    dma = pltpu.SemaphoreType.DMA
    return pl.pallas_call(
        functools.partial(kernel, groups, slabs),
        out_shape=jax.ShapeDtypeStruct((rows, nj), BF16),
        in_specs=[pl.BlockSpec(memory_space=pl.ANY)] * 4,
        out_specs=pl.BlockSpec(memory_space=pltpu.VMEM),
        scratch_shapes=[
            pltpu.VMEM((groups, rows, norb), BF16),
            pltpu.VMEM((2, slabs * count, norb), BF16),
            pltpu.VMEM((2, slabs * count, nj), BF16),
            pltpu.VMEM((groups, rows, slabs * count), BF16),
            pltpu.VMEM((rows, slabs * count), BF16),
            pltpu.VMEM((2, rows, nj), BF16),
            pltpu.VMEM((groups, 1, count), jnp.int32),
            pltpu.VMEM((2 * count, groups * rows), BF16),
            pltpu.VMEM((2 * count, 2 * rows), BF16),
            pltpu.VMEM((2 * count, early + nj), BF16),
            pltpu.VMEM((2 * count, early + nj), BF16),
            pltpu.VMEM((2 * count, early + nj), BF16),
            pltpu.VMEM((count, norb - early), BF16),
            pltpu.VMEM((count, norb - early), BF16),
            pltpu.VMEM((3, rows, nj), BF16),
            pltpu.VMEM((2, rows, nj), BF16),
            pltpu.VMEM((2, rows, nj), BF16),
            pltpu.VMEM((groups, rows, nj), F32),
            dma((3 + groups,)),
            dma((len(SORTS),)),
            dma((transfers,)),
            dma((2,)),
            dma((pieces + 2, 2 * lanes - 1)),
            dma((2,)),
        ],
        compiler_params=pltpu.CompilerParams(
            collective_id=0, has_side_effects=True, vmem_limit_bytes=63 * 1024 * 1024),
    )(orbitals, targets, points, potential)


def solution(mesh):
    placed = (
        P(("grid", "ipts"), None),
        P(("grid", "ipts"), None),
        P("ipts", "grid"),
        P("grid", "ipts"),
    )
    return jax.shard_map(
        local, mesh=mesh, in_specs=placed, out_specs=P(("grid", "ipts"), None), check_vma=False
    )
```

time: 97 us -> 86.2 us (0.89)
  Pallas kernels: 95.2 us -> 84.4 us
    pallas_call x1, Pallas kernels: 95.2 us -> 84.4 us  [local(): pl.pallas_call(functools.partial(kernel, groups, slabs), out_shape=jax.Sh...]
where the time goes in v2:
time: 86.2 us; the launch traced here: 86.1 us
  Pallas kernels  84.4 us (98%)
  local copies, waits for them, and re-layouts  1.67 us (2%)
    pallas_call x1, Pallas kernels, local(): pl.pallas_call(functools.partial(kernel, groups, slabs), out_shape=jax.Sh...  84.4 us

profile of v2, /device:TPU:0, one launch (start us, length us, event | category | flops | bytes accessed | tf_op | source)
XLA Modules:
  0.0 86.1 jit_solution(15451533857188156887)
XLA Ops:
  0.0 84.4 %shard_map.46 = bf16[512,256]{1,0:T(8,128)(2,1)} custom-call(bf16[512,1024]{1,0:T(8,128)(2,1)} %orbitals.1, bf16[512,256]{1,0:T(8,128)(2,1)} %targets.1, s32[1,128]{1,0:T(1,128)} %points.1, bf16[2048,1024]{1,0:T(8,128)(2,1)} %potential.1), custom_call_target="tpu_custom_call" | custom-call | tf_op jit(solution)/shard_map/pallas_call | solution.py:427
  84.4 1.7 %copy.6 = bf16[512,256]{1,0:T(8,128)(2,1)} copy(bf16[512,256]{1,0:T(8,128)(2,1)} %shard_map.46) | data formatting | bytes 524288

commit v3 on v2

--- a/solution.py
+++ b/solution.py
@@ -1,4 +1,5 @@
 import functools
+import math
 
 import jax
 import jax.numpy as jnp
@@ -11,7 +12,10 @@
 LANES = 128
 WIDTH = 1024
 SPLIT = 2
-EARLY = 4
+EARLY = (3, 8)
+DIRECT = 2
+LOANS = 8
+ROOM, MOST = 8 << 20, 63 << 20
 SORTS = ("index", "slab", "targets", "lent", "near", "early", "values", "target values", "sums")
 F32, BF16 = jnp.float32, jnp.bfloat16
 
@@ -45,11 +49,12 @@
     partner = g + 1 - 2 * core
     bits = [1 << n for n in range(lanes.bit_length() - 1)]
     orders = (bits, bits[::-1])
-    early = norb // EARLY
+    early = norb * EARLY[0] // EARLY[1]
     tail = norb - early
     pieces = tail // LANES
     sub = rows // SPLIT
     quarter = sub // 2
+    loan = rows // LOANS
     width = min(WIDTH, total)
     names = Names(recv_sem.shape[0])
 
@@ -84,34 +89,53 @@
             pltpu.make_async_copy(view, view, send_sem.at[SORTS.index(sort)]).wait()
 
     wide = pieces + 1
+    direct = max(pieces - DIRECT, 1)
 
     def pass_to(block, item, way, target):
-        recv = partner_recv.at[item // wide] if way is None else plane_recv.at[item, way - 1]
+        recv = partner_recv.at[item // wide] if way is None else plane_recv.at[item, way]
         pltpu.make_async_remote_copy(
             src_ref=block, dst_ref=block, send_sem=plane_send.at[item // wide], recv_sem=recv,
             device_id={"grid": target, "ipts": z}, device_id_type=MESH).start()
 
+    routed = [mask for mask in range(1, lanes) if mask not in bits]
+
+    def way_of(mask, slot):
+        if mask in bits:
+            return bits.index(mask)
+        return len(bits) + slot * len(routed) + routed.index(mask)
+
     def ways(mask, slots):
         if mask in bits:
-            return [(mask, None)]
-        return [(mask + slot * lanes, slot) for slot in range(slots)]
+            return [(way_of(mask, None), None)]
+        return [(way_of(mask, slot), slot) for slot in range(slots)]
 
     def spread(item, view, slots):
         for bit in bits:
-            pass_to(view(None, place(g)), item, bit, flipped(bit, core))
+            pass_to(view(None, place(g)), item, way_of(bit, None), flipped(bit, core))
         pass_to(view(None, place(g)), item, None, partner)
+
+    def spread_straight(item, view):
+        for mask in range(1, lanes):
+            pass_to(view(0, place(g)), item, way_of(mask, 0), flipped(mask, core))
+        pass_to(view(0, place(g)), item, None, partner)
+
+    def hand_over(item, view):
+        for mask in range(1, lanes):
+            block = view(0, place(flipped(mask, core)))
+            pltpu.make_async_copy(block, block, plane_recv.at[item, way_of(mask, 0)]).wait()
+            pass_to(block, item, None, partner)
 
     def forward(item, view, slots, single):
         masks = [m for m in range(1, lanes) if (m in bits) == single]
         for mask in sorted(masks, key=lambda m: m.bit_count()):
             for way, slot in ways(mask, slots):
                 block = view(slot, place(flipped(mask, core)))
-                pltpu.make_async_copy(block, block, plane_recv.at[item, way - 1]).wait()
+                pltpu.make_async_copy(block, block, plane_recv.at[item, way]).wait()
                 for n in range(slots) if slot is None else (slot,):
                     order = orders[n]
                     top = max(order.index(bit) for bit in bits if mask & bit)
                     for bit in order[top + 1:]:
-                        pass_to(view(n, place(flipped(mask, core))), item, (mask | bit) + n * lanes, flipped(bit, core))
+                        pass_to(view(n, place(flipped(mask, core))), item, way_of(mask | bit, n), flipped(bit, core))
                 pass_to(block, item, None, partner)
 
     def all_of(blocks, pick):
@@ -162,9 +186,12 @@
     greet(g, inward)
     pl.when(q > 0)(lambda: greet(g, outward))
     greet(partner, z)
-    for bit in bits:
-        greet(flipped(bit, core), z)
-    pl.semaphore_wait(barrier, len(bits) + 2 + q)
+    for mask in range(1, lanes):
+        if mask in bits:
+            greet(flipped(mask, core), z)
+        else:
+            pl.when(q == 0)(lambda mask=mask: greet(flipped(mask, core), z))
+    pl.semaphore_wait(barrier, jnp.where(q == 0, lanes + 1, len(bits) + 3))
 
     halves = range(SPLIT)
 
@@ -195,10 +222,13 @@
         send(1, "targets", "targets", targets, target_rows.at[0], inward)
         for k in range(pieces):
             send(1, ("end", k), "slab", orbitals.at[:, cols(k)], slab.at[0, :, cols(k)], inward)
-        for half in halves:
-            part = pl.ds(pl.multiple_of(where(1) * rows + half * sub, sub), sub)
-            send(1, ("lent", half), "lent", potential.at[part, :], lent.at[pl.ds(half * sub, sub), :], inward)
-
+
+        def lend(n):
+            part = pl.ds(pl.multiple_of(where(1) * rows + n * loan, loan), loan)
+            send(1, ("lent", n), "lent", potential.at[part, :], lent.at[pl.ds(n * loan, loan), :], inward)
+
+        for n in range(LOANS - 2):
+            lend(n)
         views = [lambda n, p: values.at[0, p, last]]
         views += [lambda n, p, k=k: values.at[0, p, cols(k)] for k in range(pieces)]
         views += [lambda n, p: target_values.at[0, p, :]]
@@ -208,35 +238,42 @@
         receive(0, "near", near_in)
         for item in (0, wide):
             receive(0, ("value", item), views[item](0, place(g)))
-            spread(item, views[item], 1)
-        before, older = [0, wide], []
+            spread_straight(item, views[item])
+        waiting = [0, wide]
         for k in range(pieces):
-            for block in (2, 3):
-                receive(0, ("out", block, k), slab.at[block, :, cols(k)])
-            found = pick(marks, (0, 2, 3), lambda block: slab[block, :, cols(k)])
-            values[0, place(g), cols(k)] = (found + near_in[:, cols(k)].astype(F32)).astype(BF16)
-            spread(k + 1, views[k + 1], 1)
-            for item in before:
-                forward(item, views[item], 1, True)
-            for item in older:
-                forward(item, views[item], 1, False)
-            before, older = [k + 1], before
-        for item in before:
-            forward(item, views[item], 1, True)
-        for item in older + before:
-            forward(item, views[item], 1, False)
+            if k < direct:
+                for block in (2, 3):
+                    receive(0, ("out", block, k), slab.at[block, :, cols(k)])
+                found = pick(marks, (0, 2, 3), lambda block: slab[block, :, cols(k)])
+                values[0, place(g), cols(k)] = (found + near_in[:, cols(k)].astype(F32)).astype(BF16)
+            else:
+                receive(0, ("value", k + 1), views[k + 1](0, place(g)))
+            spread_straight(k + 1, views[k + 1])
+            while len(waiting) > 1:
+                item = waiting.pop(0)
+                hand_over(item, views[item])
+            waiting.append(k + 1)
+        for item in waiting:
+            hand_over(item, views[item])
         own_targets.wait()
         for copy in own_weights:
             copy.wait()
         gathered(0)
+        for k in range(direct, pieces):
+            for block in (2, 3):
+                receive(0, ("out", block, k), slab.at[block, :, cols(k)])
         for block in (3, 2):
             for half in halves:
                 part = pl.ds(half * sub, sub)
-                receive(0, ("out rows", block, half), slab.at[block, part, last])
+                for n in quarters[half]:
+                    receive(0, ("out rows", block, n), slab.at[block, few(n), last])
                 leaving[block - 2, part, :] = contribution(block, half, 0, weights.at[block]).astype(BF16)
                 for n in quarters[half]:
                     send(1, ("sum", block, n), "sums", leaving.at[block - 2, few(n), :],
                          arriving.at[block - 2, few(n), :], inward)
+                if (block, half) == (3, 0):
+                    lend(LOANS - 2)
+        lend(LOANS - 1)
         for half in halves:
             kept[0, pl.ds(half * sub, sub), :] = contribution(0, half, 0, weights.at[0])
         for n in range(2 * SPLIT):
@@ -257,10 +294,12 @@
         def own(k):
             send(1, ("own", k), "slab", orbitals.at[:, cols(k)], slab.at[2, :, cols(k)], inward)
 
-        own(0)
+        first = min(pieces, 3)
+        for k in range(first):
+            own(k)
         receive(1, "index", index.at[0])
         send(1, "index end", "index", index.at[0], index.at[3], inward)
-        for k in range(1, pieces):
+        for k in range(first, pieces):
             own(k)
 
         def relay(block, k):
@@ -277,7 +316,7 @@
         mark(hot, (1, 0), range(groups))
         own_rows.wait()
         near_out[...] = jnp.dot(
-            hot[pl.ds(count, count), pl.ds(rows, rows)], slab[1, :, pl.ds(0, tail)],
+            hot[pl.ds(count, count), pl.ds(rows, rows)], slab[1, :, pl.ds(0, direct * LANES)],
             preferred_element_type=F32).astype(BF16)
         send(0, "near", "near", near_out, near_in, outward)
         ahead = max(pieces - 2, 0)
@@ -288,76 +327,81 @@
         mark(far_hot, (2, 3), (0, 1))
         own_targets.wait()
         receive(1, "early rows", slab.at[0, :, last])
-        receive(1, "targets", target_rows.at[0])
-        early_out[:, pl.ds(0, early)] = pick(far_hot, (0, 1), lambda b: slab[b, :, last]).astype(BF16)
-        early_out[:, pl.ds(early, nj)] = pick(far_hot, (0, 1), lambda b: target_rows[b]).astype(BF16)
-        send(1, "early", "early", early_out, early_in, inward)
-        early_near[:, pl.ds(0, early)] = pick(hot, (0, 1), lambda b: slab[b, :, last]).astype(BF16)
-        early_near[:, pl.ds(early, nj)] = pick(hot, (0, 1), lambda b: target_rows[b]).astype(BF16)
+        orbital_part, target_part = pl.ds(0, early), pl.ds(early, nj)
+        early_out[:, orbital_part] = pick(far_hot, (0, 1), lambda b: slab[b, :, last]).astype(BF16)
+        send(1, "early", "early", early_out.at[:, orbital_part], early_in.at[:, orbital_part], inward)
+        early_near[:, orbital_part] = pick(hot, (0, 1), lambda b: slab[b, :, last]).astype(BF16)
         for k in range(ahead, pieces):
             relay_own(k)
-        ready = min(pieces, 3)
-        for k in range(ready):
-            cross(k)
+        receive(1, "targets", target_rows.at[0])
+        early_out[:, target_part] = pick(far_hot, (0, 1), lambda b: target_rows[b]).astype(BF16)
+        send(1, "early targets", "early", early_out.at[:, target_part], early_in.at[:, target_part], inward)
+        early_near[:, target_part] = pick(hot, (0, 1), lambda b: target_rows[b]).astype(BF16)
+        ready = 1
+        cross(0)
 
         views = [lambda n, p: values.at[both if n is None else n, p, last]]
         views += [lambda n, p, k=k: values.at[both if n is None else n, p, cols(k)] for k in range(pieces)]
         views += [lambda n, p: target_values.at[both if n is None else n, p, :]]
 
-        receive(1, "early", early_in)
-        found = early_near[...].astype(F32) + early_in[...].astype(F32)
+        def found_early(part):
+            return early_near[:, part].astype(F32) + early_in[:, part].astype(F32)
+
+        receive(1, "early", early_in.at[:, orbital_part])
+        found = found_early(orbital_part)
         for n in range(2):
-            part = slice(n * count, (n + 1) * count)
-            values[n, place(g), last] = found[part, :early].astype(BF16)
-            target_values[n, place(g), :] = found[part, early:].astype(BF16)
+            values[n, place(g), last] = found[n * count:(n + 1) * count].astype(BF16)
         send(0, ("value", 0), "values", values.at[1, place(g), last], values.at[0, place(g), last], outward)
+        spread(0, views[0], 2)
+        if pieces > 1:
+            ready = 2
+            cross(1)
+        receive(1, "early targets", early_in.at[:, target_part])
+        found = found_early(target_part)
+        for n in range(2):
+            target_values[n, place(g), :] = found[n * count:(n + 1) * count].astype(BF16)
         send(0, ("value", wide), "target values", target_values.at[1, place(g), :],
              target_values.at[0, place(g), :], outward)
-        spread(0, views[0], 2)
         spread(wide, views[wide], 2)
 
         def rows_in():
             for block in (0, 1):
-                for half in halves:
-                    part = pl.ds(half * sub, sub)
-                    send(1, ("rows in", 3 - block, half), "slab", slab.at[block, part, last],
-                         slab.at[3 - block, part, last], inward)
-
-        before, older = [0, wide], []
+                for n in range(2 * SPLIT):
+                    send(1, ("rows in", 3 - block, n), "slab", slab.at[block, few(n), last],
+                         slab.at[3 - block, few(n), last], inward)
+
+        batches = [[0, wide]] + [[k + 1] for k in range(pieces)]
+
+        def onward(n, single):
+            for item in batches[n]:
+                forward(item, views[item], 2, single)
+
         for k in range(pieces):
-            while ready < min(pieces, 5 + k):
+            while ready < min(pieces, 3 + k):
                 cross(ready)
                 ready += 1
                 if ready == pieces:
                     rows_in()
             receive(1, ("end in", k), slab.at[3, :, cols(k)])
-            relay(3, k)
+            if k < direct:
+                relay(3, k)
             found = pick(hot, range(groups), lambda b: slab[b, :, cols(k)])
             for n in range(2):
                 values[n, place(g), cols(k)] = found[n * count:(n + 1) * count].astype(BF16)
+            if k >= direct:
+                send(0, ("value", k + 1), "values", values.at[1, place(g), cols(k)],
+                     values.at[0, place(g), cols(k)], outward)
+                relay(3, k)
             spread(k + 1, views[k + 1], 2)
-            for item in before:
-                forward(item, views[item], 2, True)
-            for item in older:
-                forward(item, views[item], 2, False)
-            before, older = [k + 1], before
-
-        def pass_on(block):
-            for half in halves:
-                part = pl.ds(half * sub, sub)
-                receive(1, ("rows in", block, half), slab.at[block, part, last])
-                send(0, ("out rows", block, half), "slab", slab.at[block, part, last],
-                     slab.at[block, part, last], outward)
-
-        pass_on(3)
-        for item in before:
-            forward(item, views[item], 2, True)
-        for item in older + before:
-            forward(item, views[item], 2, False)
-        pass_on(2)
-        for copy in own_weights:
-            copy.wait()
-        gathered(both)
+            if k > 0:
+                onward(k - 1, True)
+            if k > 1:
+                onward(k - 2, False)
+
+        def pass_on(block, n):
+            receive(1, ("rows in", block, n), slab.at[block, few(n), last])
+            send(0, ("out rows", block, n), "slab", slab.at[block, few(n), last],
+                 slab.at[block, few(n), last], outward)
 
         def keep(block, half, slot, kernel_rows):
             part = pl.ds(half * sub, sub)
@@ -380,23 +424,40 @@
         def near(half):
             part = pl.ds(half * sub, sub)
             keep(1, half, 0, weights.at[1])
-            receive(1, ("lent", half), lent.at[part, :])
+            for n in range(half * LOANS // SPLIT, (half + 1) * LOANS // SPLIT):
+                receive(1, ("lent", n), lent.at[pl.ds(n * loan, loan), :])
             kept[1, part, :] += contribution(1, half, 1, lent)
 
-        for block in (3, 2):
-            for half in halves:
-                keep(block, half, 0, weights.at[block])
-                if half > 0:
-                    sums(block, half - 1)
-            if block == 2:
-                for half in halves:
-                    keep(0, half, 0, weights.at[0])
-            for half in halves:
-                if block == 2:
-                    end_sums(half)
-            sums(block, SPLIT - 1)
-        for half in halves:
-            near(half)
+        onward(pieces - 1, True)
+        onward(pieces - 2, False)
+        pass_on(3, 0)
+        pass_on(3, 1)
+        onward(pieces, True)
+        onward(pieces - 1, False)
+        pass_on(3, 2)
+        onward(pieces, False)
+        for copy in own_weights:
+            copy.wait()
+        gathered(both)
+        keep(3, 0, 0, weights.at[3])
+        pass_on(3, 3)
+        keep(3, 1, 0, weights.at[3])
+        pass_on(2, 0)
+        keep(0, 0, 0, weights.at[0])
+        pass_on(2, 1)
+        keep(2, 0, 0, weights.at[2])
+        pass_on(2, 2)
+        sums(3, 0)
+        pass_on(2, 3)
+        keep(2, 1, 0, weights.at[2])
+        keep(0, 1, 0, weights.at[0])
+        sums(3, 1)
+        end_sums(0)
+        sums(2, 0)
+        end_sums(1)
+        near(0)
+        sums(2, 1)
+        near(1)
         for n in range(2 * SPLIT):
             receive(1, ("sum in", 2, n), crossing.at[1, few(n), :])
             out[few(n), :] = (-(kept[1, few(n), :] + crossing[1, few(n), :].astype(F32))).astype(out.dtype)
@@ -404,7 +465,7 @@
         left("slab", slab)
         left("near", near_out)
         left("early", early_out)
-        left("values", values.at[0, pl.ds(0, count), last])
+        left("values", values.at[0, pl.ds(0, count), pl.ds(direct * LANES, norb - direct * LANES)])
         left("target values", target_values.at[0, pl.ds(0, count), :])
         left("sums", leaving)
         passed(both)
@@ -419,45 +480,51 @@
     rows, norb = orbitals.shape
     nj = targets.shape[1]
     count = points.shape[1]
-    early = norb // EARLY
+    early = norb * EARLY[0] // EARLY[1]
     pieces = (norb - early) // LANES
-    transfers = 6 + 3 * pieces + 11 * SPLIT
+    transfers = 7 + 3 * pieces + 12 * SPLIT + LOANS
     lanes = slabs // 2
+    doublings = lanes.bit_length() - 1
     dma = pltpu.SemaphoreType.DMA
+    buffers = [
+        pltpu.VMEM((groups, rows, norb), BF16),
+        pltpu.VMEM((2, slabs * count, norb), BF16),
+        pltpu.VMEM((2, slabs * count, nj), BF16),
+        pltpu.VMEM((groups, rows, slabs * count), BF16),
+        pltpu.VMEM((rows, slabs * count), BF16),
+        pltpu.VMEM((2, rows, nj), BF16),
+        pltpu.VMEM((groups, 1, count), jnp.int32),
+        pltpu.VMEM((2 * count, groups * rows), BF16),
+        pltpu.VMEM((2 * count, 2 * rows), BF16),
+        pltpu.VMEM((2 * count, early + nj), BF16),
+        pltpu.VMEM((2 * count, early + nj), BF16),
+        pltpu.VMEM((2 * count, early + nj), BF16),
+        pltpu.VMEM((count, max(pieces - DIRECT, 1) * LANES), BF16),
+        pltpu.VMEM((count, max(pieces - DIRECT, 1) * LANES), BF16),
+        pltpu.VMEM((3, rows, nj), BF16),
+        pltpu.VMEM((2, rows, nj), BF16),
+        pltpu.VMEM((2, rows, nj), BF16),
+        pltpu.VMEM((groups, rows, nj), F32),
+    ]
+    size = sum(math.prod(b.shape) * jnp.dtype(b.dtype).itemsize for b in buffers)
+    limit = min(size + ROOM, MOST)
+    held = [pltpu.with_memory_space_constraint(x, pltpu.HBM) for x in (orbitals, targets, points, potential)]
     return pl.pallas_call(
         functools.partial(kernel, groups, slabs),
         out_shape=jax.ShapeDtypeStruct((rows, nj), BF16),
         in_specs=[pl.BlockSpec(memory_space=pl.ANY)] * 4,
         out_specs=pl.BlockSpec(memory_space=pltpu.VMEM),
-        scratch_shapes=[
-            pltpu.VMEM((groups, rows, norb), BF16),
-            pltpu.VMEM((2, slabs * count, norb), BF16),
-            pltpu.VMEM((2, slabs * count, nj), BF16),
-            pltpu.VMEM((groups, rows, slabs * count), BF16),
-            pltpu.VMEM((rows, slabs * count), BF16),
-            pltpu.VMEM((2, rows, nj), BF16),
-            pltpu.VMEM((groups, 1, count), jnp.int32),
-            pltpu.VMEM((2 * count, groups * rows), BF16),
-            pltpu.VMEM((2 * count, 2 * rows), BF16),
-            pltpu.VMEM((2 * count, early + nj), BF16),
-            pltpu.VMEM((2 * count, early + nj), BF16),
-            pltpu.VMEM((2 * count, early + nj), BF16),
-            pltpu.VMEM((count, norb - early), BF16),
-            pltpu.VMEM((count, norb - early), BF16),
-            pltpu.VMEM((3, rows, nj), BF16),
-            pltpu.VMEM((2, rows, nj), BF16),
-            pltpu.VMEM((2, rows, nj), BF16),
-            pltpu.VMEM((groups, rows, nj), F32),
+        scratch_shapes=buffers + [
             dma((3 + groups,)),
             dma((len(SORTS),)),
             dma((transfers,)),
             dma((2,)),
-            dma((pieces + 2, 2 * lanes - 1)),
+            dma((pieces + 2, doublings + 2 * (lanes - 1 - doublings))),
             dma((2,)),
         ],
         compiler_params=pltpu.CompilerParams(
-            collective_id=0, has_side_effects=True, vmem_limit_bytes=63 * 1024 * 1024),
-    )(orbitals, targets, points, potential)
+            collective_id=0, has_side_effects=True, vmem_limit_bytes=limit),
+    )(*held)
 
 
 def solution(mesh):

time: 86.2 us -> 74.8 us (0.87); the launches traced: 86.1 us -> 73.6 us
  Pallas kernels: 84.4 us -> 72.9 us
  local copies, waits for them, and re-layouts: 1.67 us -> 0.71 us
    pallas_call x1, Pallas kernels: 84.4 us -> 72.9 us  [local(): pl.pallas_call(functools.partial(kernel, groups, slabs), out_shape=jax.Sh...]
    unnamed x1, local copies, waits for them, and re-layouts: 1.67 us -> 0.71 us
where the time goes in v3:
time: 74.8 us; the launch traced here: 73.6 us
  Pallas kernels  72.9 us (97%)
    pallas_call x1, Pallas kernels, local(): pl.pallas_call(functools.partial(kernel, groups, slabs), out_shape=jax.Sh...  72.9 us

profile of v3, /device:TPU:0, one launch (start us, length us, event | category | flops | bytes accessed | tf_op | source)
XLA Modules:
  0.0 73.6 jit_solution(2336692266219022963)
XLA Ops:
  0.0 72.9 %shard_map.46 = bf16[512,256]{1,0:T(8,128)(2,1)S(1)} custom-call(bf16[512,1024]{1,0:T(8,128)(2,1)} %orbitals.1, bf16[512,256]{1,0:T(8,128)(2,1)} %targets.1, s32[1,128]{1,0:T(1,128)} %points.1, bf16[2048,1024]{1,0:T(8,128)(2,1)} %potential.1), custom_call_target="tpu_custom_call" | custom-call | tf_op jit(solution)/shard_map/pallas_call | solution.py:512
  72.9 0.7 copy.6

commit v4 on v3

--- a/solution.py
+++ b/solution.py
@@ -13,8 +13,8 @@
 WIDTH = 1024
 SPLIT = 2
 EARLY = (3, 8)
-DIRECT = 2
-LOANS = 8
+DIRECT = 1
+LOANS = 16
 ROOM, MOST = 8 << 20, 63 << 20
 SORTS = ("index", "slab", "targets", "lent", "near", "early", "values", "target values", "sums")
 F32, BF16 = jnp.float32, jnp.bfloat16
@@ -33,7 +33,7 @@
 
 def kernel(groups, slabs, orbitals, targets, points, potential, out,
            slab, values, target_values, weights, lent, target_rows, index, hot, far_hot,
-           early_out, early_near, early_in, near_out, near_in, leaving, arriving, crossing, kept,
+           early_out, early_near, early_in, near_out, near_in, leaving, arriving, crossing, kept, head,
            local_sem, send_sem, recv_sem, plane_send, plane_recv, partner_recv):
     g = lax.axis_index("grid")
     z = lax.axis_index("ipts")
@@ -150,8 +150,7 @@
         for n, view in enumerate(all_of(slabs - 1, pick)):
             pltpu.make_async_copy(view, view, plane_send.at[n]).wait()
 
-    def contribution(block, half, slot, kernel_rows):
-        part = pl.ds(half * sub, sub)
+    def contribution(block, part, slot, kernel_rows):
         acc = None
         for start in range(0, total, width):
             some = pl.ds(start, width)
@@ -162,6 +161,17 @@
             term = jnp.dot(weighted, target_values[slot, some, :], preferred_element_type=F32)
             acc = term if acc is None else acc + term
         return acc
+
+    def begin(block, part):
+        head[...] = lax.dot_general(
+            slab[block, part, pl.ds(0, tail)], values[0, :, pl.ds(0, tail)], (((1,), (1,)), ((), ())),
+            preferred_element_type=F32)
+
+    def complete(block, part, kernel_rows):
+        products = head[...] + lax.dot_general(
+            slab[block, part, last], values[0, :, last], (((1,), (1,)), ((), ())), preferred_element_type=F32)
+        weighted = (kernel_rows[part, :].astype(F32) * products).astype(BF16)
+        return jnp.dot(weighted, target_values[0], preferred_element_type=F32)
 
     own_rows = pltpu.make_async_copy(orbitals, slab.at[q], local_sem.at[0])
     own_targets = pltpu.make_async_copy(targets, target_rows.at[q], local_sem.at[1])
@@ -225,7 +235,7 @@
 
         def lend(n):
             part = pl.ds(pl.multiple_of(where(1) * rows + n * loan, loan), loan)
-            send(1, ("lent", n), "lent", potential.at[part, :], lent.at[pl.ds(n * loan, loan), :], inward)
+            send(1, ("lent", n * SPLIT // LOANS), "lent", potential.at[part, :], lent.at[pl.ds(n * loan, loan), :], inward)
 
         for n in range(LOANS - 2):
             lend(n)
@@ -262,20 +272,23 @@
         for k in range(direct, pieces):
             for block in (2, 3):
                 receive(0, ("out", block, k), slab.at[block, :, cols(k)])
+        begin(3, few(0))
         for block in (3, 2):
-            for half in halves:
-                part = pl.ds(half * sub, sub)
-                for n in quarters[half]:
-                    receive(0, ("out rows", block, n), slab.at[block, few(n), last])
-                leaving[block - 2, part, :] = contribution(block, half, 0, weights.at[block]).astype(BF16)
-                for n in quarters[half]:
-                    send(1, ("sum", block, n), "sums", leaving.at[block - 2, few(n), :],
-                         arriving.at[block - 2, few(n), :], inward)
-                if (block, half) == (3, 0):
+            for n in range(2 * SPLIT):
+                receive(0, ("out rows", block, n), slab.at[block, few(n), last])
+                leaving[block - 2, few(n), :] = complete(block, few(n), weights.at[block]).astype(BF16)
+                send(1, ("sum", block, n), "sums", leaving.at[block - 2, few(n), :],
+                     arriving.at[block - 2, few(n), :], inward)
+                if n + 1 < 2 * SPLIT:
+                    begin(block, few(n + 1))
+                elif block == 3:
+                    begin(2, few(0))
+                if block == 2 and n == SPLIT - 1:
                     lend(LOANS - 2)
         lend(LOANS - 1)
         for half in halves:
-            kept[0, pl.ds(half * sub, sub), :] = contribution(0, half, 0, weights.at[0])
+            part = pl.ds(half * sub, sub)
+            kept[0, part, :] = contribution(0, part, 0, weights.at[0])
         for n in range(2 * SPLIT):
             receive(0, ("end sum", n), arriving.at[0, few(n), :])
             out[few(n), :] = (-(kept[0, few(n), :] + arriving[0, few(n), :].astype(F32))).astype(out.dtype)
@@ -395,8 +408,8 @@
             spread(k + 1, views[k + 1], 2)
             if k > 0:
                 onward(k - 1, True)
-            if k > 1:
-                onward(k - 2, False)
+            if k > 2:
+                onward(k - 3, False)
 
         def pass_on(block, n):
             receive(1, ("rows in", block, n), slab.at[block, few(n), last])
@@ -405,7 +418,7 @@
 
         def keep(block, half, slot, kernel_rows):
             part = pl.ds(half * sub, sub)
-            kept[block, part, :] = contribution(block, half, slot, kernel_rows)
+            kept[block, part, :] = contribution(block, part, slot, kernel_rows)
 
         def sums(block, half):
             for n in quarters[half]:
@@ -424,17 +437,18 @@
         def near(half):
             part = pl.ds(half * sub, sub)
             keep(1, half, 0, weights.at[1])
-            for n in range(half * LOANS // SPLIT, (half + 1) * LOANS // SPLIT):
-                receive(1, ("lent", n), lent.at[pl.ds(n * loan, loan), :])
-            kept[1, part, :] += contribution(1, half, 1, lent)
-
+            receive(1, ("lent", half), lent.at[part, :])
+            kept[1, part, :] += contribution(1, part, 1, lent)
+
+        pass_on(3, 0)
         onward(pieces - 1, True)
+        for n in range(max(pieces - 3, 0), pieces - 2):
+            onward(n, False)
+        pass_on(3, 1)
         onward(pieces - 2, False)
-        pass_on(3, 0)
-        pass_on(3, 1)
         onward(pieces, True)
+        pass_on(3, 2)
         onward(pieces - 1, False)
-        pass_on(3, 2)
         onward(pieces, False)
         for copy in own_weights:
             copy.wait()
@@ -482,7 +496,7 @@
     count = points.shape[1]
     early = norb * EARLY[0] // EARLY[1]
     pieces = (norb - early) // LANES
-    transfers = 7 + 3 * pieces + 12 * SPLIT + LOANS
+    transfers = 7 + 3 * pieces + 13 * SPLIT
     lanes = slabs // 2
     doublings = lanes.bit_length() - 1
     dma = pltpu.SemaphoreType.DMA
@@ -505,6 +519,7 @@
         pltpu.VMEM((2, rows, nj), BF16),
         pltpu.VMEM((2, rows, nj), BF16),
         pltpu.VMEM((groups, rows, nj), F32),
+        pltpu.VMEM((rows // (2 * SPLIT), slabs * count), F32),
     ]
     size = sum(math.prod(b.shape) * jnp.dtype(b.dtype).itemsize for b in buffers)
     limit = min(size + ROOM, MOST)

time: 74.8 us -> 71.4 us (0.955); the launches traced: 73.6 us -> 71.2 us
  Pallas kernels: 72.9 us -> 70.5 us
    pallas_call x1, Pallas kernels: 72.9 us -> 70.5 us  [local(): pl.pallas_call(functools.partial(kernel, groups, slabs), out_shape=jax.Sh...]
where the time goes in v4:
time: 71.4 us; the launch traced here: 71.2 us
  Pallas kernels  70.5 us (99%)
    pallas_call x1, Pallas kernels, local(): pl.pallas_call(functools.partial(kernel, groups, slabs), out_shape=jax.Sh...  70.5 us

profile of v4, /device:TPU:0, one launch (start us, length us, event | category | flops | bytes accessed | tf_op | source)
XLA Modules:
  0.0 71.2 jit_solution(15536652487104227795)
XLA Ops:
  0.0 70.5 %shard_map.46 = bf16[512,256]{1,0:T(8,128)(2,1)S(1)} custom-call(bf16[512,1024]{1,0:T(8,128)(2,1)} %orbitals.1, bf16[512,256]{1,0:T(8,128)(2,1)} %targets.1, s32[1,128]{1,0:T(1,128)} %points.1, bf16[2048,1024]{1,0:T(8,128)(2,1)} %potential.1), custom_call_target="tpu_custom_call" | custom-call | tf_op jit(solution)/shard_map/pallas_call | solution.py:527
  70.5 0.7 copy.6

commit v5 on v4

--- a/solution.py
+++ b/solution.py
@@ -179,7 +179,7 @@
     own_weights = [
         pltpu.make_async_copy(
             potential.at[pl.ds(pl.multiple_of(where(block) * rows, rows), rows), :], weights.at[block],
-            local_sem.at[3 + block])
+            local_sem.at[3])
         for block in range(groups)
     ]
     own_points.start()
@@ -210,6 +210,11 @@
     def few(n):
         return pl.ds(n * quarter, quarter)
 
+    def parts(block, n):
+        if block == 2 and n == 2 * SPLIT - 1:
+            return [pl.ds(n * quarter + m * (quarter // 2), quarter // 2) for m in range(2)]
+        return [few(n)]
+
     def mark(ref, marked, blocks):
         spot = lax.broadcasted_iota(jnp.int32, (count, LANES), 1)
         for n, group in enumerate(marked):
@@ -228,10 +233,11 @@
     def end():
         own_points.wait()
         send(1, "index", "index", index.at[0], index.at[0], inward)
-        send(1, "early rows", "slab", orbitals.at[:, last], slab.at[0, :, last], inward)
+        own_rows.wait()
+        send(1, "early rows", "slab", slab.at[0, :, last], slab.at[0, :, last], inward)
         send(1, "targets", "targets", targets, target_rows.at[0], inward)
         for k in range(pieces):
-            send(1, ("end", k), "slab", orbitals.at[:, cols(k)], slab.at[0, :, cols(k)], inward)
+            send(1, ("end", k), "slab", slab.at[0, :, cols(k)], slab.at[0, :, cols(k)], inward)
 
         def lend(n):
             part = pl.ds(pl.multiple_of(where(1) * rows + n * loan, loan), loan)
@@ -244,7 +250,6 @@
         views += [lambda n, p: target_values.at[0, p, :]]
         marks = hot.at[pl.ds(0, count), :]
         mark(marks, (0,), (0, 2, 3))
-        own_rows.wait()
         receive(0, "near", near_in)
         for item in (0, wide):
             receive(0, ("value", item), views[item](0, place(g)))
@@ -266,8 +271,7 @@
         for item in waiting:
             hand_over(item, views[item])
         own_targets.wait()
-        for copy in own_weights:
-            copy.wait()
+        pltpu.make_async_copy(weights, weights, local_sem.at[3]).wait()
         gathered(0)
         for k in range(direct, pieces):
             for block in (2, 3):
@@ -277,8 +281,9 @@
             for n in range(2 * SPLIT):
                 receive(0, ("out rows", block, n), slab.at[block, few(n), last])
                 leaving[block - 2, few(n), :] = complete(block, few(n), weights.at[block]).astype(BF16)
-                send(1, ("sum", block, n), "sums", leaving.at[block - 2, few(n), :],
-                     arriving.at[block - 2, few(n), :], inward)
+                for part in parts(block, n):
+                    send(1, ("sum", block, part.start), "sums", leaving.at[block - 2, part, :],
+                         arriving.at[block - 2, part, :], inward)
                 if n + 1 < 2 * SPLIT:
                     begin(block, few(n + 1))
                 elif block == 3:
@@ -305,13 +310,14 @@
         send(1, "index in", "index", index.at[1], index.at[2], inward)
 
         def own(k):
-            send(1, ("own", k), "slab", orbitals.at[:, cols(k)], slab.at[2, :, cols(k)], inward)
-
+            send(1, ("own", k), "slab", slab.at[1, :, cols(k)], slab.at[2, :, cols(k)], inward)
+
+        own_rows.wait()
         first = min(pieces, 3)
         for k in range(first):
             own(k)
         receive(1, "index", index.at[0])
-        send(1, "index end", "index", index.at[0], index.at[3], inward)
+        send(1, "index in", "index", index.at[0], index.at[3], inward)
         for k in range(first, pieces):
             own(k)
 
@@ -327,7 +333,6 @@
             send(1, ("end in", k), "slab", slab.at[0, :, cols(k)], slab.at[3, :, cols(k)], inward)
 
         mark(hot, (1, 0), range(groups))
-        own_rows.wait()
         near_out[...] = jnp.dot(
             hot[pl.ds(count, count), pl.ds(rows, rows)], slab[1, :, pl.ds(0, direct * LANES)],
             preferred_element_type=F32).astype(BF16)
@@ -335,8 +340,7 @@
         ahead = max(pieces - 2, 0)
         for k in range(ahead):
             relay_own(k)
-        receive(1, "index in", index.at[2])
-        receive(1, "index end", index.at[3])
+        receive(1, "index in", index.at[pl.ds(2, 2)])
         mark(far_hot, (2, 3), (0, 1))
         own_targets.wait()
         receive(1, "early rows", slab.at[0, :, last])
@@ -422,15 +426,16 @@
 
         def sums(block, half):
             for n in quarters[half]:
-                receive(1, ("sum", block, n), arriving.at[block - 2, few(n), :])
-                leaving[block - 2, few(n), :] = (
-                    kept[block, few(n), :] + arriving[block - 2, few(n), :].astype(F32)).astype(BF16)
-                send(1, ("sum in", block, n), "sums", leaving.at[block - 2, few(n), :],
-                     crossing.at[3 - block, few(n), :], inward)
+                for part in parts(block, n):
+                    receive(1, ("sum", block, part.start), arriving.at[block - 2, part, :])
+                    leaving[block - 2, part, :] = (
+                        kept[block, part, :] + arriving[block - 2, part, :].astype(F32)).astype(BF16)
+                    send(1, ("sum in", block, part.start), "sums", leaving.at[block - 2, part, :],
+                         crossing.at[3 - block, part, :], inward)
 
         def end_sums(half):
             for n in quarters[half]:
-                receive(1, ("sum in", 3, n), crossing.at[0, few(n), :])
+                receive(1, ("sum in", 3, few(n).start), crossing.at[0, few(n), :])
                 leaving[2, few(n), :] = (kept[0, few(n), :] + crossing[0, few(n), :].astype(F32)).astype(BF16)
                 send(0, ("end sum", n), "sums", leaving.at[2, few(n), :], arriving.at[0, few(n), :], outward)
 
@@ -450,8 +455,7 @@
         pass_on(3, 2)
         onward(pieces - 1, False)
         onward(pieces, False)
-        for copy in own_weights:
-            copy.wait()
+        pltpu.make_async_copy(weights, weights, local_sem.at[3]).wait()
         gathered(both)
         keep(3, 0, 0, weights.at[3])
         pass_on(3, 3)
@@ -473,8 +477,9 @@
         sums(2, 1)
         near(1)
         for n in range(2 * SPLIT):
-            receive(1, ("sum in", 2, n), crossing.at[1, few(n), :])
-            out[few(n), :] = (-(kept[1, few(n), :] + crossing[1, few(n), :].astype(F32))).astype(out.dtype)
+            for part in parts(2, n):
+                receive(1, ("sum in", 2, part.start), crossing.at[1, part, :])
+                out[part, :] = (-(kept[1, part, :] + crossing[1, part, :].astype(F32))).astype(out.dtype)
         left("index", index.at[both])
         left("slab", slab)
         left("near", near_out)
@@ -496,7 +501,7 @@
     count = points.shape[1]
     early = norb * EARLY[0] // EARLY[1]
     pieces = (norb - early) // LANES
-    transfers = 7 + 3 * pieces + 13 * SPLIT
+    transfers = 7 + 3 * pieces + 13 * SPLIT + 1
     lanes = slabs // 2
     doublings = lanes.bit_length() - 1
     dma = pltpu.SemaphoreType.DMA
@@ -530,7 +535,7 @@
         in_specs=[pl.BlockSpec(memory_space=pl.ANY)] * 4,
         out_specs=pl.BlockSpec(memory_space=pltpu.VMEM),
         scratch_shapes=buffers + [
-            dma((3 + groups,)),
+            dma((4,)),
             dma((len(SORTS),)),
             dma((transfers,)),
             dma((2,)),

time: 71.4 us -> 71.1 us (level)
  no operation moved by 1% of the time
where the time goes in v5:
time: 71.1 us; the launch traced here: 70.9 us
  Pallas kernels  70.2 us (99%)
    pallas_call x1, Pallas kernels, local(): pl.pallas_call(functools.partial(kernel, groups, slabs), out_shape=jax.Sh...  70.2 us

profile of v5, /device:TPU:0, one launch (start us, length us, event | category | flops | bytes accessed | tf_op | source)
XLA Modules:
  0.0 70.9 jit_solution(8543456828038640892)
XLA Ops:
  0.0 70.2 %shard_map.46 = bf16[512,256]{1,0:T(8,128)(2,1)S(1)} custom-call(bf16[512,1024]{1,0:T(8,128)(2,1)} %orbitals.1, bf16[512,256]{1,0:T(8,128)(2,1)} %targets.1, s32[1,128]{1,0:T(1,128)} %points.1, bf16[2048,1024]{1,0:T(8,128)(2,1)} %potential.1), custom_call_target="tpu_custom_call" | custom-call | tf_op jit(solution)/shard_map/pallas_call | solution.py:532
  70.2 0.7 copy.6
